TPU v7x, 32 devices: a whole 2x2x4 slice. The times are simulated.
32 devices in a mesh: member: 4 (over y, core), patch: 8 (over z, x).
Axes of the slice: x: 2, y: 2, z: 4, core: 2. Of those that a mesh axis runs over, the one named last changes fastest.
Arguments:
- kernel_rows: bfloat16 [2048, 2048], P('patch'), as said below
- row_scale: float32 [2048], P('patch'), may hold values from 0.3 to 1
- self_stiffness: float32 [2048], P('patch'), may hold values from 1 to 3
- base_stress: float32 [2048], P('patch'), may hold values from 0.5 to 2.5
- friction_rate: float32 [2048], P('patch'), may hold values from 0.5 to 2
- damping: float32 [2048], P('patch'), may hold values from 0.5 to 2
- deficit_start: float32 [24, 2048], P('member', 'patch'), may hold values from -3 to 3
- state_start: float32 [24, 2048], P('member', 'patch'), may hold values from -1 to 1
- obs_rate: float32 [2048], P('patch'), may hold values from -6 to 6
- obs_precision: float32 [2048], P('patch'), may hold values from 0.2 to 2
Outputs:
- analysis: float32 [3, 24, 8, 256], P(None, None, 'patch', 'member')
Inputs may be any that keep to these rules, and one draw needn't show every extreme that they name: `kernel_rows`: entries are independent with mean zero and root mean square of order 2048 ** -0.5 times a per-row factor.
All inputs are finite; a program needn't handle non-finite values.
Results may differ from a plain program's by a relative error of at most 0.0006.
Values may be sent and summed in bfloat16 or wider, within the bound.
A program may use at most 64 MiB of HBM per device.

v0:
```python
import jax
import jax.numpy as jnp
from jax import lax
from jax.sharding import PartitionSpec as P

STEPS = 2
NEWTON = 4
NS_ITERS = 6
MARGIN = 8


time_step = 0.25
plate_rate = 1.0


def padded_2(cells, sides, width):
    for axis, dim in sides:
        count = lax.axis_size(axis)
        ends = count - 1
        head = lax.slice_in_dim(cells, 0, width, axis=dim)
        tail = lax.slice_in_dim(cells, cells.shape[dim] - width, cells.shape[dim], axis=dim)
        cells = jnp.concatenate(
            [
                lax.ppermute(tail, axis, [(i, (i + 1) % count) for i in range(ends)]),
                cells,
                lax.ppermute(head, axis, [((i + 1) % count, i) for i in range(ends)]),
            ],
            axis=dim,
        )
    return cells


def inverse_sinh(value):
    magnitude = jnp.abs(value)
    result = jnp.log(magnitude + jnp.sqrt(magnitude * magnitude + 1.0))
    return jnp.where(value < 0, -result, result)


def slip_rate(stress, state_log, guess, friction_rate, damping):
    factor = 0.5 * jnp.exp(state_log / friction_rate)
    velocity = guess
    for _ in range(NEWTON):
        scaled = factor * velocity
        residual = friction_rate * inverse_sinh(scaled) + damping * velocity - stress
        derivative = friction_rate * factor / jnp.sqrt(1.0 + scaled * scaled) + damping
        velocity = velocity - residual / derivative
    return velocity


def analyse(local_state, rate_window, obs_window):
    ensemble = rate_window.shape[0]
    window_width = rate_window.shape[1]
    sub_block = local_state.shape[2]
    margin = (window_width - sub_block) // 2
    highest = lax.Precision.HIGHEST
    mean_rate = jnp.mean(rate_window, axis=0)
    anomalies = rate_window - mean_rate[None, :]
    innovation = obs_window[0] - mean_rate
    distance = jnp.abs(
        jnp.arange(sub_block, dtype=jnp.int32)[:, None]
        + margin
        - jnp.arange(window_width, dtype=jnp.int32)[None, :]
    ).astype(jnp.float32)
    tapering = jnp.where(distance <= margin, jnp.exp(-0.5 * (distance / margin) ** 2), 0.0)
    weights = tapering * obs_window[1][None, :]
    weighted = anomalies[None, :, :] * weights[:, None, :]
    cross_terms = jnp.einsum("imj,nj->imn", weighted, anomalies, precision=highest)
    drive_terms = jnp.einsum("imj,j->im", weighted, innovation, precision=highest)
    identity = jnp.eye(ensemble, dtype=jnp.float32)
    scaling = ensemble - 1.0 + jnp.trace(cross_terms, axis1=1, axis2=2)
    root_part = ((ensemble - 1.0) * identity[None] + cross_terms) / scaling[:, None, None]
    inverse_root = jnp.broadcast_to(identity, root_part.shape)
    for _ in range(NS_ITERS):
        mixing = 1.5 * identity[None] - 0.5 * jnp.matmul(inverse_root, root_part, precision=highest)
        root_part = jnp.matmul(root_part, mixing, precision=highest)
        inverse_root = jnp.matmul(mixing, inverse_root, precision=highest)
    half_step = jnp.einsum("imn,in->im", inverse_root, drive_terms, precision=highest)
    mean_weight = (
        jnp.einsum("imn,in->im", inverse_root, half_step, precision=highest) / scaling[:, None]
    )
    spread = jnp.sqrt(ensemble - 1.0) * inverse_root / jnp.sqrt(scaling)[:, None, None]
    combined = spread + mean_weight[:, :, None]
    state_mean = jnp.mean(local_state, axis=1)
    state_spread = local_state - state_mean[:, None, :]
    return state_mean[:, None, :] + jnp.einsum(
        "vmi,imk->vki", state_spread, combined, precision=highest
    )


def body(
    kernel_rows,
    row_scale,
    self_stiffness,
    base_stress,
    friction_rate,
    damping,
    deficit_start,
    state_start,
    obs_rate,
    obs_precision,
):
    groups = lax.axis_size("member")
    own_rows = kernel_rows.shape[0]
    members = deficit_start.shape[0]
    sub_block = own_rows // groups
    margin = MARGIN

    def coupling(deficit):
        rounded = deficit.astype(jnp.bfloat16)
        summed = lax.dot_general(
            lax.all_gather(rounded, "patch", axis=1, tiled=True),
            kernel_rows,
            (((1,), (1,)), ((), ())),
            preferred_element_type=jnp.float32,
        )
        return base_stress + self_stiffness * deficit + row_scale * summed

    def tendency(deficit, state_log, guess):
        velocity = slip_rate(coupling(deficit), state_log, guess, friction_rate, damping)
        return (plate_rate - velocity, jnp.exp(-state_log) - jnp.abs(velocity), velocity)

    deficit = deficit_start
    state_log = state_start
    velocity = jnp.zeros_like(deficit_start)
    for _ in range(STEPS):
        deficit_zero, state_zero = (deficit, state_log)
        change, state_change, velocity = tendency(deficit_zero, state_zero, velocity)
        deficit_one = deficit_zero + time_step * change
        state_one = state_zero + time_step * state_change
        change, state_change, velocity = tendency(deficit_one, state_one, velocity)
        deficit_two = 0.75 * deficit_zero + 0.25 * (deficit_one + time_step * change)
        state_two = 0.75 * state_zero + 0.25 * (state_one + time_step * state_change)
        change, state_change, velocity = tendency(deficit_two, state_two, velocity)
        deficit = deficit_zero / 3.0 + 2.0 / 3.0 * (deficit_two + time_step * change)
        state_log = state_zero / 3.0 + 2.0 / 3.0 * (state_two + time_step * state_change)
    velocity = slip_rate(coupling(deficit), state_log, velocity, friction_rate, damping)
    stacked = jnp.stack([deficit, state_log, velocity])
    observed = jnp.stack([obs_rate, obs_precision])
    group_index = lax.axis_index("member")
    joined = jnp.concatenate([velocity, observed], axis=0)
    padded = padded_2(joined, (("patch", 1),), margin)
    padded_rate = padded[:members]
    padded_obs = padded[members:]
    lower_rim = padded_rate[:, :own_rows].reshape(members, groups, sub_block)[:, :, :margin]
    middle = padded_rate[:, margin : margin + own_rows].reshape(members, groups, sub_block)
    upper_rim = padded_rate[:, 2 * margin : 2 * margin + own_rows].reshape(
        members, groups, sub_block
    )[:, :, sub_block - margin :]
    windows = jnp.concatenate([lower_rim, middle, upper_rim], axis=2)[None]
    states = stacked[:2].reshape(2, members, groups, sub_block)
    moved_states, moved_windows = (
        lax.all_to_all(states, "member", split_axis=2, concat_axis=1, tiled=True),
        lax.all_to_all(windows, "member", split_axis=2, concat_axis=1, tiled=True),
    )
    rate_window = moved_windows[0, :, 0, :]
    local_state = jnp.concatenate(
        [moved_states[:, :, 0, :], rate_window[None, :, margin : margin + sub_block]], axis=0
    )
    obs_window = lax.dynamic_slice_in_dim(
        padded_obs, group_index * sub_block, sub_block + 2 * margin, 1
    )
    analysis = analyse(local_state, rate_window, obs_window)
    return analysis[:, :, None, :]


def solution(mesh):
    return jax.shard_map(
        body,
        mesh=mesh,
        in_specs=(
            P("patch", None),
            P("patch"),
            P("patch"),
            P("patch"),
            P("patch"),
            P("patch"),
            P("member", "patch"),
            P("member", "patch"),
            P("patch"),
            P("patch"),
        ),
        out_specs=P(None, None, "patch", "member"),
        check_vma=False,
    )
```

profile of v0, /device:TPU:0, one launch (start us, length us, event | category | flops | bytes accessed | tf_op | source)
XLA Modules:
  0.0 277.0 jit_solution(11388620996137495112)
XLA Ops:
  0.0 0.8 convert_element_type.35
  0.8 32.6 %all_gather.21 = bf16[6,2048]{1,0:T(8,128)(2,1)S(1)} all-gather(bf16[6,256]{1,0:T(8,128)(2,1)S(1)} %convert_element_type.35), channel_id=1, replica_groups=mesh['member'=4,'patch'=8] {'patch'}, dimensions={1}, use_global_device_ids=true | all-gather | bytes 27648 | tf_op jit(solution)/shard_map/all_gather | solution.py:111
  33.4 0.6 copy-done.6
  34.6 30.6 %all_gather.22 = bf16[6,2048]{1,0:T(8,128)(2,1)S(1)} all-gather(bf16[6,256]{1,0:T(8,128)(2,1)S(1)} %get-tuple-element.17), channel_id=1, replica_groups=mesh['member'=4,'patch'=8] {'patch'}, dimensions={1}, use_global_device_ids=true | all-gather | bytes 27648 | tf_op jit(solution)/shard_map/all_gather | solution.py:111
  65.2 0.5 fusion.188
  65.6 30.6 %all_gather.23 = bf16[6,2048]{1,0:T(8,128)(2,1)S(1)} all-gather(bf16[6,256]{1,0:T(8,128)(2,1)S(1)} %get-tuple-element.19), channel_id=1, replica_groups=mesh['member'=4,'patch'=8] {'patch'}, dimensions={1}, use_global_device_ids=true | all-gather | bytes 27648 | tf_op jit(solution)/shard_map/all_gather | solution.py:111
  96.3 0.5 fusion.191
  96.7 30.6 %all_gather.24 = bf16[6,2048]{1,0:T(8,128)(2,1)S(1)} all-gather(bf16[6,256]{1,0:T(8,128)(2,1)S(1)} %get-tuple-element.7), channel_id=1, replica_groups=mesh['member'=4,'patch'=8] {'patch'}, dimensions={1}, use_global_device_ids=true | all-gather | bytes 27648 | tf_op jit(solution)/shard_map/all_gather | solution.py:111
  127.3 0.5 fusion.179
  127.8 30.6 %all_gather.25 = bf16[6,2048]{1,0:T(8,128)(2,1)S(1)} all-gather(bf16[6,256]{1,0:T(8,128)(2,1)S(1)} %get-tuple-element.22), channel_id=1, replica_groups=mesh['member'=4,'patch'=8] {'patch'}, dimensions={1}, use_global_device_ids=true | all-gather | bytes 27648 | tf_op jit(solution)/shard_map/all_gather | solution.py:111
  158.4 0.5 fusion.189
  158.9 30.6 %all_gather.26 = bf16[6,2048]{1,0:T(8,128)(2,1)S(1)} all-gather(bf16[6,256]{1,0:T(8,128)(2,1)S(1)} %get-tuple-element.24), channel_id=1, replica_groups=mesh['member'=4,'patch'=8] {'patch'}, dimensions={1}, use_global_device_ids=true | all-gather | bytes 27648 | tf_op jit(solution)/shard_map/all_gather | solution.py:111
  189.5 0.5 fusion.190
  190.0 30.6 %all_gather.27 = bf16[6,2048]{1,0:T(8,128)(2,1)S(1)} all-gather(bf16[6,256]{1,0:T(8,128)(2,1)S(1)} %get-tuple-element.5), channel_id=1, replica_groups=mesh['member'=4,'patch'=8] {'patch'}, dimensions={1}, use_global_device_ids=true | all-gather | bytes 27648 | tf_op jit(solution)/shard_map/all_gather | solution.py:111
  221.3 0.5 copy-done.8
  221.8 3.4 %collective-permute-start = (f32[8,8]{1,0:T(8,128)S(1)}, f32[8,8]{1,0:T(8,128)S(1)}, u32[]{:S(2)}, u32[]{:S(2)}) collective-permute-start(f32[8,8]{1,0:T(8,128)S(1)} %get-tuple-element.13), channel_id=1, source_target_pairs={{0,1},{1,2},{2,3},{3,4},{4,5},{5,6},{6,7},{8,9},{9,10},{10,11},{11... | collective-permute-start | bytes 776 | tf_op jit(solution)/shard_map/ppermute | solution.py:24
  225.2 1.3 collective-permute-start.1
  226.9 0.7 reshape.124
  227.6 3.1 %collective-permute-done.1 = f32[8,8]{1,0:T(8,128)S(1)} collective-permute-done((f32[8,8]{1,0:T(8,128)S(1)}, f32[8,8]{1,0:T(8,128)S(1)}, u32[]{:S(2)}, u32[]{:S(2)}) %collective-permute-start.1) | collective-permute-done | bytes 288 | tf_op jit(solution)/shard_map/ppermute | solution.py:26
  231.2 0.6 copy.52
  231.8 3.3 %all-to-all-start.1 = ((f32[1,6,4,80]{3,0,1,2:T(1,128)}), f32[1,6,4,80]{3,0,1,2:T(1,128)S(1)}, u32[]{:S(2)}, u32[]{:S(2)}) async-start(f32[1,6,4,80]{3,0,1,2:T(1,128)} %copy.52), calls=%async_computation.1 | async-start | bytes 24576 | tf_op jit(solution)/shard_map/all_to_all | solution.py:153
  235.2 3.7 %all-to-all-done.1 = f32[1,6,4,80]{3,0,1,2:T(1,128)S(1)} async-done(((f32[1,6,4,80]{3,0,1,2:T(1,128)}), f32[1,6,4,80]{3,0,1,2:T(1,128)S(1)}, u32[]{:S(2)}, u32[]{:S(2)}) %all-to-all-start.1) | async-done | bytes 7712 | tf_op jit(solution)/shard_map/all_to_all | solution.py:153
  238.9 3.4 %all-to-all-start = ((f32[4,1,768]{2,1,0:T(1,128)}), f32[4,1,768]{2,1,0:T(1,128)S(1)}, u32[]{:S(2)}, u32[]{:S(2)}) async-start(f32[4,1,768]{2,1,0:T(1,128)} %reshape.124), calls=%async_computation | async-start | bytes 24576 | tf_op jit(solution)/shard_map/all_to_all | solution.py:152
  242.4 2.0 select_reduce_fusion
  244.9 1.4 fusion.5
  246.2 1.4 fusion.194
  247.6 1.4 fusion.29
  249.0 1.4 fusion.4
  250.4 1.4 fusion.196
  251.8 1.4 fusion.195
  253.1 1.4 fusion.3
  254.5 1.6 fusion.198
  256.1 1.4 fusion.197
  257.5 1.4 fusion.2
  258.9 1.4 fusion.200
  260.3 1.4 fusion.199
  261.7 1.4 fusion.1
  263.1 1.4 fusion.202
  264.4 1.4 fusion.201
  265.8 1.9 fusion.8
  267.7 1.7 fusion
  269.4 1.4 fusion.203
  270.9 1.3 convolution_bitcast_fusion.1
  272.2 1.3 fusion.204
  273.7 0.5 broadcast.301
  274.3 0.7 reduce.3
  275.3 1.0 fusion.7
  276.3 0.7 copy.61
  (63 shorter events, 3.3 us)
Async XLA Ops:
  0.0 33.4 %copy-start = (bf16[256,2048]{1,0:T(8,128)(2,1)S(1)}, bf16[256,2048]{1,0:T(8,128)(2,1)}, u32[]{:S(2)}) copy-start(bf16[256,2048]{1,0:T(8,128)(2,1)} %param.10) | copy-start | bytes 3145732
  0.8 32.6 %copy-start.3 = (f32[256]{0:T(256)S(1)}, f32[256]{0:T(256)}, u32[]{:S(2)}) copy-start(f32[256]{0:T(256)} %param.15) | copy-start | bytes 3076
  0.8 32.6 %copy-start.4 = (f32[256]{0:T(256)S(1)}, f32[256]{0:T(256)}, u32[]{:S(2)}) copy-start(f32[256]{0:T(256)} %param.14) | copy-start | bytes 3076
  0.8 32.6 %copy-start.1 = (f32[6,256]{1,0:T(8,128)S(1)}, f32[6,256]{1,0:T(8,128)}, u32[]{:S(2)}) copy-start(f32[6,256]{1,0:T(8,128)} %param.16) | copy-start | bytes 18436
  0.8 32.6 %copy-start.2 = (f32[6,256]{1,0:T(8,128)S(1)}, f32[6,256]{1,0:T(8,128)}, u32[]{:S(2)}) copy-start(f32[6,256]{1,0:T(8,128)} %param.17) | copy-start | bytes 18436
  33.4 0.7 copy-start.6
  33.4 0.7 copy-start.7
  33.4 0.7 copy-start.5
  220.6 0.7 copy-start.9
  221.1 0.7 copy-start.8
  221.8 5.7 %collective-permute-start = (f32[8,8]{1,0:T(8,128)S(1)}, f32[8,8]{1,0:T(8,128)S(1)}, u32[]{:S(2)}, u32[]{:S(2)}) collective-permute-start(f32[8,8]{1,0:T(8,128)S(1)} %get-tuple-element.13), channel_id=1, source_target_pairs={{0,1},{1,2},{2,3},{3,4},{4,5},{5,6},{6,7},{8,9},{9,10},{10,11},{11... | collective-permute-start | bytes 776 | tf_op jit(solution)/shard_map/ppermute | solution.py:24
  225.2 5.5 %collective-permute-start.1 = (f32[8,8]{1,0:T(8,128)S(1)}, f32[8,8]{1,0:T(8,128)S(1)}, u32[]{:S(2)}, u32[]{:S(2)}) collective-permute-start(f32[8,8]{1,0:T(8,128)S(1)} %get-tuple-element.14), channel_id=1, source_target_pairs={{1,0},{2,1},{3,2},{4,3},{5,4},{6,5},{7,6},{9,8},{10,9},{11,10},{12... | collective-permute-start | bytes 776 | tf_op jit(solution)/shard_map/ppermute | solution.py:26
  231.8 7.1 %all-to-all-start.1 = ((f32[1,6,4,80]{3,0,1,2:T(1,128)}), f32[1,6,4,80]{3,0,1,2:T(1,128)S(1)}, u32[]{:S(2)}, u32[]{:S(2)}) async-start(f32[1,6,4,80]{3,0,1,2:T(1,128)} %copy.52), calls=%async_computation.1 | async-start | bytes 24576 | tf_op jit(solution)/shard_map/all_to_all | solution.py:153
  238.9 34.8 %all-to-all-start = ((f32[4,1,768]{2,1,0:T(1,128)}), f32[4,1,768]{2,1,0:T(1,128)S(1)}, u32[]{:S(2)}, u32[]{:S(2)}) async-start(f32[4,1,768]{2,1,0:T(1,128)} %reshape.124), calls=%async_computation | async-start | bytes 24576 | tf_op jit(solution)/shard_map/all_to_all | solution.py:152
where the time goes:
time: 278 us; the launch traced here: 277 us
  blocking collectives  216 us (78%)
  matrix products  34.7 us (12%)
  starting transfers between devices  11.3 us (4%)
  waiting for transfers between devices  6.85 us (2%)
  local copies, waits for them, and re-layouts  5.24 us (2%)
    all_gather x7, blocking collectives, coupling(): lax.all_gather(rounded, 'patch', axis=1, tiled=True)  216 us
    dot_general x6, matrix products, analyse(): jnp.matmul(inverse_root, root_part, precision=highest)  8.54 us
    dot_general x6, matrix products, analyse(): inverse_root = jnp.matmul(mixing, inverse_root, precision=highest)  8.23 us
    dot_general x5, matrix products, analyse(): root_part = jnp.matmul(root_part, mixing, precision=highest)  7.12 us
  transfers between devices with their start and end apart: 4, of which 2 were waited for; matrix products, arithmetic and copies ran while one was open for 12% of the time, Pallas kernels for 0%

commit v1 on v0

v1 whole, which is shorter than its diff:
```python
import functools
import math

import jax
import jax.numpy as jnp
from jax import lax
from jax.experimental import pallas as pl
from jax.experimental.pallas import tpu as pltpu
from jax.sharding import PartitionSpec as P

STEPS = 2
NEWTON = 4
NS_ITERS = 6
MARGIN = 8
LANES = 128
TILE = 8

time_step = 0.25
plate_rate = 1.0

MESH = pl.DeviceIdType.MESH


def slip_rate(stress, state_log, guess, friction, inverse_friction, damping):
    factor = 0.5 * jnp.exp(state_log * inverse_friction)
    slope = friction * factor
    velocity = guess
    for _ in range(NEWTON):
        scaled = factor * velocity
        square = 1.0 + scaled * scaled
        inverse = lax.rsqrt(square)
        grown = jnp.log(jnp.abs(scaled) + square * inverse)
        grown = jnp.where(scaled < 0, -grown, grown)
        residual = friction * grown + damping * velocity - stress
        velocity = velocity - residual / (slope * inverse + damping)
    return velocity


def forecast_kernel(
    groups,
    count,
    kernel_hbm,
    row_scale_ref,
    stiffness_ref,
    base_ref,
    friction_ref,
    damping_ref,
    deficit_ref,
    state_ref,
    obs_rate_ref,
    obs_precision_ref,
    fields_out,
    kernel_ref,
    start_ref,
    gathered,
    packed,
    landed,
    lower,
    upper,
    load_sem,
    gather_send,
    gather_recv,
    move_send,
    move_recv,
    rim_send,
    rim_recv,
):
    member = lax.axis_index("member")
    patch = lax.axis_index("patch")
    members, own = deficit_ref.shape
    rows = start_ref.shape[1]
    sub_block = own // groups
    last = groups - 1

    load = pltpu.make_async_copy(kernel_hbm, kernel_ref, load_sem)
    load.start()

    lower[...] = jnp.zeros_like(lower)
    upper[...] = jnp.zeros_like(upper)
    start_ref[...] = jnp.zeros_like(start_ref)
    start_ref[0, 0:members] = deficit_ref[...]
    start_ref[1, 0:members] = state_ref[...]

    barrier = pltpu.get_barrier_semaphore()

    def greet(where):
        pl.semaphore_signal(barrier, inc=1, device_id=where, device_id_type=MESH)

    for shift in range(1, count):
        greet((member, lax.rem(patch + shift, count)))
    for shift in range(1, groups):
        greet((lax.rem(member + shift, groups), patch))

    after = lax.rem(patch + 1, count)
    before = lax.rem(patch + count - 1, count)
    greet((0, after))
    greet((last, before))

    @pl.when(member == 0)
    def _():
        for other in range(groups):
            greet((other, before))

    @pl.when(member == last)
    def _():
        for other in range(groups):
            greet((other, after))

    at_end = 1 - lax.div(member + last, groups) + lax.div(member + 1, groups)
    pl.semaphore_wait(barrier, count + groups + groups * at_end)

    row_scale = row_scale_ref[...]
    stiffness = stiffness_ref[...]
    base = base_ref[...]
    friction = friction_ref[...]
    damping = damping_ref[...]
    inverse_friction = 1.0 / friction

    stage = [0]

    def stress_of(deficit):
        slot = stage[0] % 2
        mine = gathered.at[slot, patch]
        gathered[slot, patch] = deficit.astype(jnp.bfloat16)
        copies = []
        for shift in range(1, count):
            copy = pltpu.make_async_remote_copy(
                src_ref=mine,
                dst_ref=mine,
                send_sem=gather_send.at[slot, shift],
                recv_sem=gather_recv.at[slot, shift],
                device_id=(member, lax.rem(patch + shift, count)),
                device_id_type=MESH,
            )
            copy.start()
            copies.append(copy)
        if stage[0] == 0:
            load.wait()
        for shift in range(1, count):
            source = gathered.at[slot, lax.rem(patch + count - shift, count)]
            pltpu.make_async_remote_copy(
                src_ref=source,
                dst_ref=source,
                send_sem=gather_send.at[slot, shift],
                recv_sem=gather_recv.at[slot, shift],
                device_id=(member, lax.rem(patch + count - shift, count)),
                device_id_type=MESH,
            ).wait_recv()
        summed = lax.dot_general(
            jnp.concatenate([gathered[slot, q] for q in range(count)], axis=1),
            kernel_ref[...],
            (((1,), (1,)), ((), ())),
            preferred_element_type=jnp.float32,
        )
        for copy in copies:
            copy.wait_send()
        stage[0] += 1
        return base + stiffness * deficit + row_scale * summed

    def rate(deficit, state_log, guess):
        return slip_rate(
            stress_of(deficit), state_log, guess, friction, inverse_friction, damping
        )

    def tendency(deficit, state_log, guess):
        velocity = rate(deficit, state_log, guess)
        return (plate_rate - velocity, jnp.exp(-state_log) - jnp.abs(velocity), velocity)

    deficit = start_ref[0]
    state_log = start_ref[1]
    velocity = jnp.zeros_like(deficit)
    for _ in range(STEPS):
        deficit_zero, state_zero = (deficit, state_log)
        change, state_change, velocity = tendency(deficit_zero, state_zero, velocity)
        deficit_one = deficit_zero + time_step * change
        state_one = state_zero + time_step * state_change
        change, state_change, velocity = tendency(deficit_one, state_one, velocity)
        deficit_two = 0.75 * deficit_zero + 0.25 * (deficit_one + time_step * change)
        state_two = 0.75 * state_zero + 0.25 * (state_one + time_step * state_change)
        change, state_change, velocity = tendency(deficit_two, state_two, velocity)
        deficit = deficit_zero / 3.0 + 2.0 / 3.0 * (deficit_two + time_step * change)
        state_log = state_zero / 3.0 + 2.0 / 3.0 * (state_two + time_step * state_change)
    velocity = rate(deficit, state_log, velocity)

    row = lax.broadcasted_iota(jnp.int32, (rows, own), 0)
    joined = jnp.where(row == members, obs_rate_ref[...], velocity)
    joined = jnp.where(row == members + 1, obs_precision_ref[...], joined)

    def window(cells, first):
        return pltpu.roll(cells, (-first) % own, 1)[:, :LANES]

    for group in range(groups):
        packed[group, 0:rows] = window(joined, group * sub_block - MARGIN)
        packed[group, rows : 2 * rows] = window(deficit, group * sub_block)
        packed[group, 2 * rows :] = window(state_log, group * sub_block)

    def move(shift):
        other = lax.rem(member + shift, groups)
        return pltpu.make_async_remote_copy(
            src_ref=packed.at[other],
            dst_ref=landed.at[shift],
            send_sem=move_send.at[shift],
            recv_sem=move_recv.at[shift],
            device_id=(other, patch),
            device_id_type=MESH,
        )

    def right_rim():
        return pltpu.make_async_remote_copy(
            src_ref=packed.at[0, 0:rows],
            dst_ref=lower.at[member],
            send_sem=rim_send.at[0],
            recv_sem=rim_recv.at[0, member],
            device_id=(0, after),
            device_id_type=MESH,
        )

    def left_rim():
        return pltpu.make_async_remote_copy(
            src_ref=packed.at[last, 0:rows],
            dst_ref=upper.at[member],
            send_sem=rim_send.at[1],
            recv_sem=rim_recv.at[1, member],
            device_id=(last, before),
            device_id_type=MESH,
        )

    right_rim().start()
    left_rim().start()

    for shift in range(1, groups):
        move(shift).start()

    landed[0] = packed[member]

    @pl.when(member == 0)
    def _():
        for other in range(groups):
            pltpu.make_async_remote_copy(
                src_ref=packed.at[0, 0:rows],
                dst_ref=lower.at[other],
                send_sem=rim_send.at[0],
                recv_sem=rim_recv.at[0, other],
                device_id=(other, before),
                device_id_type=MESH,
            ).wait_recv()

    @pl.when(member == last)
    def _():
        for other in range(groups):
            pltpu.make_async_remote_copy(
                src_ref=packed.at[0, 0:rows],
                dst_ref=upper.at[other],
                send_sem=rim_send.at[1],
                recv_sem=rim_recv.at[1, other],
                device_id=(other, after),
                device_id_type=MESH,
            ).wait_recv()

    for shift in range(1, groups):
        move(shift).wait_recv()

    lane = lax.broadcasted_iota(jnp.int32, (rows, LANES), 1)
    below = jnp.logical_and(lane < MARGIN, member == 0)
    above = jnp.logical_and(lane >= MARGIN + sub_block, member == last)
    start = jnp.logical_and(below, patch == 0)
    end = jnp.logical_and(above, patch == count - 1)
    outside = jnp.logical_or(start, jnp.logical_or(end, lane >= sub_block + 2 * MARGIN))
    for other in range(groups):
        held = landed[lax.rem(member - other + groups, groups)]
        cells = jnp.where(below, lower[other], held[0:rows])
        cells = jnp.where(above, upper[other], cells)
        cells = jnp.where(outside, 0.0, cells)
        fields_out[other, 0] = cells
        fields_out[other, 1] = held[rows : 2 * rows]
        fields_out[other, 2] = held[2 * rows :]

    for shift in range(1, groups):
        move(shift).wait_send()

    right_rim().wait_send()
    left_rim().wait_send()


def analysis_kernel(members, sub_block, fields_ref, out_ref, cross, mixing, kept, halfway):
    groups = fields_ref.shape[0]
    ensemble = groups * members
    split = LANES // sub_block
    per = ensemble // split
    extra = kept.shape[0] - per
    step = 24

    lane_row = lax.broadcasted_iota(jnp.int32, (1, LANES), 1)
    part = lane_row // sub_block

    def stacked(which):
        return jnp.concatenate(
            [fields_ref[g, which, 0:members] for g in range(groups)], axis=0
        )

    rates = stacked(0)
    observed = fields_ref[0, 0, members : members + 2]
    mean_rate = jnp.sum(rates, axis=0, keepdims=True) / ensemble
    anomalies = rates - mean_rate
    innovation = observed[0:1] - mean_rate
    weighted = anomalies * observed[1:2]

    source = lax.broadcasted_iota(jnp.int32, (LANES, LANES), 0)
    target = lax.broadcasted_iota(jnp.int32, (LANES, LANES), 1) % sub_block
    distance = jnp.abs(target + MARGIN - source).astype(jnp.float32)
    tapering = jnp.where(distance <= MARGIN, jnp.exp(-0.5 * (distance / MARGIN) ** 2), 0.0)

    def smooth(cells):
        return lax.dot_general(
            cells,
            tapering,
            (((1,), (0,)), ((), ())),
            precision=lax.Precision.HIGHEST,
            preferred_element_type=jnp.float32,
        )

    drive = smooth(weighted * innovation)
    trace = jnp.zeros((1, LANES), jnp.float32)
    for first in range(0, ensemble, step):
        products = jnp.concatenate(
            [weighted * anomalies[m : m + 1] for m in range(first, first + step)], axis=0
        )
        smoothed = smooth(products).reshape(step, ensemble, LANES)
        cross[first : first + step] = smoothed
        for m in range(step):
            trace = trace + smoothed[m, first + m : first + m + 1]
    scaling = ensemble - 1.0 + trace
    inverse_scaling = 1.0 / scaling

    column = lax.broadcasted_iota(jnp.int32, (ensemble, LANES), 0)

    def unit(m):
        return jnp.where(column == m, 1.0, 0.0)

    for m in range(ensemble):
        root = ((ensemble - 1.0) * unit(m) + cross[m]) * inverse_scaling
        mixing[m] = 1.5 * unit(m) - 0.5 * root
        cross[m] = root
    for r in range(per):
        root = cross[r]
        for g in range(1, split):
            root = jnp.where(part == g, cross[g * per + r], root)
        kept[r] = root

    fields = [stacked(1), stacked(2), pltpu.roll(rates, LANES - MARGIN, 1)]
    means = [jnp.sum(field, axis=0, keepdims=True) / ensemble for field in fields]
    vectors = [field - mean for field, mean in zip(fields, means)]
    for e in range(extra):
        filled = jnp.zeros((ensemble, LANES), jnp.float32)
        for t in range(e * split, min(e * split + split, 4)):
            g = t % split
            if t == 3:
                cells = drive
            else:
                cells = vectors[t]
                if g:
                    cells = pltpu.roll(cells, g * sub_block, 1)
            filled = jnp.where(part == g, cells, filled)
        kept[per + e] = filled

    def product(left, lo, hi, store):
        for first in range(0, ensemble, step):

            def some(base, sums):
                for k in range(TILE):
                    row = mixing[base + k, first : first + step]
                    sums = [
                        total + left[lo + i, pl.ds(base + k, 1)] * row
                        for i, total in enumerate(sums)
                    ]
                return sums

            sums = [jnp.zeros((step, LANES), jnp.float32) for _ in range(hi - lo)]
            if ensemble <= step:
                for base in range(0, ensemble, TILE):
                    sums = some(base, sums)
            else:
                sums = lax.fori_loop(
                    0, ensemble // TILE, lambda b, s: some(b * TILE, s), sums
                )
            for i, total in enumerate(sums):
                store(lo + i, first, total)

    def into(target):
        def store(i, first, total):
            target[i, first : first + step] = total

        return store

    def remix():
        for r in range(per):
            cells = kept[r]
            if split == 2:
                other = pltpu.roll(cells, sub_block, 1)
                spread = [jnp.where(part == 0, cells, other), jnp.where(part == 0, other, cells)]
            else:
                spread = []
                for g in range(split):
                    one = jnp.where(part == g, cells, 0.0)
                    width = sub_block
                    while width < LANES:
                        one = one + pltpu.roll(one, width, 1)
                        width *= 2
                    spread.append(one)
            for g in range(split):
                m = g * per + r
                mixing[m] = 1.5 * unit(m) - 0.5 * spread[g]

    def iterate(_, carry):
        product(kept, 0, per + extra, into(halfway))
        for e in range(extra):
            kept[per + e] = halfway[per + e]
        product(halfway, 0, per, into(kept))
        remix()
        return carry

    lax.fori_loop(0, NS_ITERS - 1, iterate, 0)
    product(kept, per, per + extra, into(halfway))

    def taken(t):
        cells = halfway[per + t // split]
        g = t % split
        return pltpu.roll(cells, LANES - g * sub_block, 1) if g else cells

    driven = taken(3)
    widening = math.sqrt(ensemble - 1.0) * lax.rsqrt(scaling)
    for v in range(3):
        spread = taken(v)
        moved = jnp.sum(spread * driven, axis=0, keepdims=True) * inverse_scaling
        result = means[v] + moved + widening * spread
        out_ref[v] = result[:, :sub_block]


def body(
    groups,
    count,
    kernel_rows,
    row_scale,
    self_stiffness,
    base_stress,
    friction_rate,
    damping,
    deficit_start,
    state_start,
    obs_rate,
    obs_precision,
):
    own, patches = kernel_rows.shape
    members = deficit_start.shape[0]
    ensemble = members * groups
    sub_block = own // groups
    rows = -(-(members + 2) // TILE) * TILE
    vmem = pl.BlockSpec(memory_space=pltpu.VMEM)
    f32 = jnp.float32

    fields = pl.pallas_call(
        functools.partial(forecast_kernel, groups, count),
        out_shape=jax.ShapeDtypeStruct((groups, 3, rows, LANES), f32),
        in_specs=[pl.BlockSpec(memory_space=pl.ANY)] + [vmem] * 9,
        out_specs=vmem,
        scratch_shapes=[
            pltpu.VMEM((own, patches), jnp.bfloat16),
            pltpu.VMEM((2, rows, own), f32),
            pltpu.VMEM((2, count, rows, own), jnp.bfloat16),
            pltpu.VMEM((groups, 3 * rows, LANES), f32),
            pltpu.VMEM((groups, 3 * rows, LANES), f32),
            pltpu.VMEM((groups, rows, LANES), f32),
            pltpu.VMEM((groups, rows, LANES), f32),
            pltpu.SemaphoreType.DMA,
            pltpu.SemaphoreType.DMA((2, count)),
            pltpu.SemaphoreType.DMA((2, count)),
            pltpu.SemaphoreType.DMA((groups,)),
            pltpu.SemaphoreType.DMA((groups,)),
            pltpu.SemaphoreType.DMA((2,)),
            pltpu.SemaphoreType.DMA((2, groups)),
        ],
        compiler_params=pltpu.CompilerParams(collective_id=0, has_side_effects=True),
    )(
        kernel_rows,
        *(
            cells.reshape(1, own)
            for cells in (row_scale, self_stiffness, base_stress, friction_rate, damping)
        ),
        deficit_start,
        state_start,
        obs_rate.reshape(1, own),
        obs_precision.reshape(1, own),
    )

    split = LANES // sub_block
    per = ensemble // split
    extra = -(-4 // split)
    analysis = pl.pallas_call(
        functools.partial(analysis_kernel, members, sub_block),
        out_shape=jax.ShapeDtypeStruct((3, ensemble, sub_block), f32),
        in_specs=[vmem],
        out_specs=vmem,
        scratch_shapes=[
            pltpu.VMEM((ensemble, ensemble, LANES), f32),
            pltpu.VMEM((ensemble, ensemble, LANES), f32),
            pltpu.VMEM((per + extra, ensemble, LANES), f32),
            pltpu.VMEM((per + extra, ensemble, LANES), f32),
        ],
    )(fields)
    return analysis[:, :, None, :]


def solution(mesh):
    return jax.shard_map(
        functools.partial(body, mesh.shape["member"], mesh.shape["patch"]),
        mesh=mesh,
        in_specs=(
            P("patch", None),
            P("patch"),
            P("patch"),
            P("patch"),
            P("patch"),
            P("patch"),
            P("member", "patch"),
            P("member", "patch"),
            P("patch"),
            P("patch"),
        ),
        out_specs=P(None, None, "patch", "member"),
        check_vma=False,
    )
```

time: 278 us -> 51.9 us (0.19)
  blocking collectives: 216 us -> 0 us
  Pallas kernels: 0 us -> 51.7 us
  matrix products: 34.7 us -> 0 us
  starting transfers between devices: 11.3 us -> 0 us
  waiting for transfers between devices: 6.85 us -> 0 us
  local copies, waits for them, and re-layouts: 5.24 us -> 0 us
    all_gather x7 -> x0, blocking collectives: 216 us -> none  [coupling(): lax.all_gather(rounded, 'patch', axis=1, tiled=True)]
    pallas_call x0 -> x2, Pallas kernels: none -> 51.7 us  [the longest x1 46.7 us: body(): pl.pallas_call(functools.partial(forecast_kernel, groups, count), out_sha...]
    dot_general x29 -> x0, matrix products: 34.7 us -> none  [the longest x6 8.54 us: analyse(): jnp.matmul(inverse_root, root_part, precision=highest)]
    all_to_all x2 -> x0, starting transfers between devices: 6.66 us -> none  [the longest x1 3.41 us: body(): lax.all_to_all(states, 'member', split_axis=2, concat_axis=1, tiled=True)]
    ppermute x2 -> x0, starting transfers between devices: 4.65 us -> none  [the longest x1 3.36 us: padded_2(): lax.ppermute(tail, axis, [(i, (i + 1) % count) for i in range(ends)])]
    all_to_all x2 -> x0, waiting for transfers between devices: 3.71 us -> none  [the longest x1 3.7 us: body(): lax.all_to_all(windows, 'member', split_axis=2, concat_axis=1, tiled=True)]
    ppermute x2 -> x0, waiting for transfers between devices: 3.14 us -> none  [the longest x1 3.14 us: padded_2(): lax.ppermute(head, axis, [((i + 1) % count, i) for i in range(ends)])]
  transfers between devices with their start and end apart: 4 -> 0, of which waited for: 2 -> 0; matrix products, arithmetic and copies ran while one was open for 12% -> 0% of each run, Pallas kernels for 0% -> 0%
where the time goes in v1:
time: 51.9 us; the launch traced here: 51.7 us
  Pallas kernels  51.7 us (100%)
    pallas_call x1, Pallas kernels, body(): pl.pallas_call(functools.partial(forecast_kernel, groups, count), out_sha...  46.7 us
    pallas_call x1, Pallas kernels, body(): pl.pallas_call(functools.partial(analysis_kernel, members, sub_block), ou...  4.93 us

profile of v1, /device:TPU:0, one launch (start us, length us, event | category | flops | bytes accessed | tf_op | source)
XLA Modules:
  0.0 51.7 jit_solution(12870358134525791635)
XLA Ops:
  0.0 46.7 %shard_map.100.fields_ref = f32[4,3,8,128]{3,2,1,0:T(8,128)} custom-call(bf16[256,2048]{1,0:T(8,128)(2,1)} %kernel_hbm.1, f32[1,256]{1,0:T(1,128)} %bitcast.10, f32[1,256]{1,0:T(1,128)} %bitcast.11, f32[1,256]{1,0:T(1,128)} %bitcast.12, f32[1,256]{1,0:T(1,128)} %bitcast.13, f32[1,256]{1,0:T(1,128)} %bitcast.14, f32[6,256]{1,0:T(8,128)} %deficit_ref.1, ...), custom_call_target="tpu_custom_call" | custom-call | tf_op jit(solution)/shard_map/pallas_call | solution.py:461
  46.7 4.9 %shard_map.101 = f32[3,24,64]{2,1,0:T(8,128)} custom-call(f32[4,3,8,128]{3,2,1,0:T(8,128)} %shard_map.100.fields_ref), custom_call_target="tpu_custom_call" | custom-call | tf_op jit(solution)/shard_map/pallas_call | solution.py:498

commit v2 on v1

--- a/solution.py
+++ b/solution.py
@@ -75,6 +75,7 @@
     load = pltpu.make_async_copy(kernel_hbm, kernel_ref, load_sem)
     load.start()
 
+    gathered[...] = jnp.zeros_like(gathered)
     lower[...] = jnp.zeros_like(lower)
     upper[...] = jnp.zeros_like(upper)
     start_ref[...] = jnp.zeros_like(start_ref)
@@ -93,21 +94,31 @@
 
     after = lax.rem(patch + 1, count)
     before = lax.rem(patch + count - 1, count)
-    greet((0, after))
-    greet((last, before))
-
-    @pl.when(member == 0)
+    has_after = 1 - lax.div(patch + 1, count)
+    has_before = lax.div(patch + count - 1, count)
+    takes_lower = (1 - lax.div(member + last, groups)) * has_before
+    takes_upper = lax.div(member + 1, groups) * has_after
+
+    @pl.when(has_after > 0)
+    def _():
+        greet((0, after))
+
+    @pl.when(has_before > 0)
+    def _():
+        greet((last, before))
+
+    @pl.when(takes_lower > 0)
     def _():
         for other in range(groups):
             greet((other, before))
 
-    @pl.when(member == last)
+    @pl.when(takes_upper > 0)
     def _():
         for other in range(groups):
             greet((other, after))
 
-    at_end = 1 - lax.div(member + last, groups) + lax.div(member + 1, groups)
-    pl.semaphore_wait(barrier, count + groups + groups * at_end)
+    rims = has_after + has_before + groups * (takes_lower + takes_upper)
+    pl.semaphore_wait(barrier, count + groups - 2 + rims)
 
     row_scale = row_scale_ref[...]
     stiffness = stiffness_ref[...]
@@ -116,42 +127,62 @@
     damping = damping_ref[...]
     inverse_friction = 1.0 / friction
 
+    def target(shift):
+        if count & (count - 1):
+            return lax.rem(patch + shift, count)
+        place = patch
+        bit = 1
+        while bit < count:
+            if shift & bit:
+                place = place + bit - 2 * bit * lax.rem(lax.div(patch, bit), 2)
+            bit *= 2
+        return place
+
+    def source(shift):
+        if count & (count - 1):
+            return lax.rem(patch + count - shift, count)
+        return target(shift)
+
     stage = [0]
 
     def stress_of(deficit):
         slot = stage[0] % 2
-        mine = gathered.at[slot, patch]
+        mine = gathered.at[slot, patch, 0:members]
         gathered[slot, patch] = deficit.astype(jnp.bfloat16)
         copies = []
-        for shift in range(1, count):
+        for shift in reversed(range(1, count)):
             copy = pltpu.make_async_remote_copy(
                 src_ref=mine,
                 dst_ref=mine,
                 send_sem=gather_send.at[slot, shift],
                 recv_sem=gather_recv.at[slot, shift],
-                device_id=(member, lax.rem(patch + shift, count)),
+                device_id=(member, target(shift)),
                 device_id_type=MESH,
             )
             copy.start()
             copies.append(copy)
         if stage[0] == 0:
             load.wait()
-        for shift in range(1, count):
-            source = gathered.at[slot, lax.rem(patch + count - shift, count)]
-            pltpu.make_async_remote_copy(
-                src_ref=source,
-                dst_ref=source,
-                send_sem=gather_send.at[slot, shift],
-                recv_sem=gather_recv.at[slot, shift],
-                device_id=(member, lax.rem(patch + count - shift, count)),
-                device_id_type=MESH,
-            ).wait_recv()
-        summed = lax.dot_general(
-            jnp.concatenate([gathered[slot, q] for q in range(count)], axis=1),
-            kernel_ref[...],
-            (((1,), (1,)), ((), ())),
-            preferred_element_type=jnp.float32,
-        )
+        summed = jnp.zeros((rows, own), jnp.float32)
+        for shift in range(count):
+            origin = source(shift)
+            if shift:
+                theirs = gathered.at[slot, origin, 0:members]
+                pltpu.make_async_remote_copy(
+                    src_ref=theirs,
+                    dst_ref=theirs,
+                    send_sem=gather_send.at[slot, shift],
+                    recv_sem=gather_recv.at[slot, shift],
+                    device_id=(member, origin),
+                    device_id_type=MESH,
+                ).wait_recv()
+            columns = pl.ds(pl.multiple_of(origin * own, LANES), own)
+            summed = summed + lax.dot_general(
+                gathered[slot, origin],
+                kernel_ref[:, columns],
+                (((1,), (1,)), ((), ())),
+                preferred_element_type=jnp.float32,
+            )
         for copy in copies:
             copy.wait_send()
         stage[0] += 1
@@ -225,15 +256,20 @@
             device_id_type=MESH,
         )
 
-    right_rim().start()
-    left_rim().start()
+    @pl.when(has_after > 0)
+    def _():
+        right_rim().start()
+
+    @pl.when(has_before > 0)
+    def _():
+        left_rim().start()
 
     for shift in range(1, groups):
         move(shift).start()
 
     landed[0] = packed[member]
 
-    @pl.when(member == 0)
+    @pl.when(takes_lower > 0)
     def _():
         for other in range(groups):
             pltpu.make_async_remote_copy(
@@ -245,7 +281,7 @@
                 device_id_type=MESH,
             ).wait_recv()
 
-    @pl.when(member == last)
+    @pl.when(takes_upper > 0)
     def _():
         for other in range(groups):
             pltpu.make_async_remote_copy(
@@ -278,8 +314,13 @@
     for shift in range(1, groups):
         move(shift).wait_send()
 
-    right_rim().wait_send()
-    left_rim().wait_send()
+    @pl.when(has_after > 0)
+    def _():
+        right_rim().wait_send()
+
+    @pl.when(has_before > 0)
+    def _():
+        left_rim().wait_send()
 
 
 def analysis_kernel(members, sub_block, fields_ref, out_ref, cross, mixing, kept, halfway):

time: 51.9 us -> 45.2 us (0.87)
  Pallas kernels: 51.7 us -> 45 us
    pallas_call x1, Pallas kernels: 46.7 us -> 40.1 us  [body(): pl.pallas_call(functools.partial(forecast_kernel, groups, count), out_sha...]
where the time goes in v2:
time: 45.2 us; the launch traced here: 45 us
  Pallas kernels  45 us (100%)
    pallas_call x1, Pallas kernels, body(): pl.pallas_call(functools.partial(forecast_kernel, groups, count), out_sha...  40.1 us
    pallas_call x1, Pallas kernels, body(): pl.pallas_call(functools.partial(analysis_kernel, members, sub_block), ou...  4.93 us

profile of v2, /device:TPU:0, one launch (start us, length us, event | category | flops | bytes accessed | tf_op | source)
XLA Modules:
  0.0 45.0 jit_solution(15418769426496674499)
XLA Ops:
  0.0 40.1 %shard_map.100.fields_ref = f32[4,3,8,128]{3,2,1,0:T(8,128)} custom-call(bf16[256,2048]{1,0:T(8,128)(2,1)} %kernel_hbm.1, f32[1,256]{1,0:T(1,128)} %bitcast.10, f32[1,256]{1,0:T(1,128)} %bitcast.11, f32[1,256]{1,0:T(1,128)} %bitcast.12, f32[1,256]{1,0:T(1,128)} %bitcast.13, f32[1,256]{1,0:T(1,128)} %bitcast.14, f32[6,256]{1,0:T(8,128)} %deficit_ref.1, ...), custom_call_target="tpu_custom_call" | custom-call | tf_op jit(solution)/shard_map/pallas_call | solution.py:502
  40.1 4.9 %shard_map.101 = f32[3,24,64]{2,1,0:T(8,128)} custom-call(f32[4,3,8,128]{3,2,1,0:T(8,128)} %shard_map.100.fields_ref), custom_call_target="tpu_custom_call" | custom-call | tf_op jit(solution)/shard_map/pallas_call | solution.py:539

commit v3 on v2

--- a/solution.py
+++ b/solution.py
@@ -40,31 +40,13 @@
     groups,
     count,
     kernel_hbm,
-    row_scale_ref,
-    stiffness_ref,
-    base_ref,
-    friction_ref,
-    damping_ref,
-    deficit_ref,
-    state_ref,
-    obs_rate_ref,
-    obs_precision_ref,
-    fields_out,
-    kernel_ref,
-    start_ref,
-    gathered,
-    packed,
-    landed,
-    lower,
-    upper,
-    load_sem,
-    gather_send,
-    gather_recv,
-    move_send,
-    move_recv,
-    rim_send,
-    rim_recv,
+    *rest,
 ):
+    sources, fields_out, held_here, rest = rest[:9], rest[9], rest[10:19], rest[19:]
+    kernel_ref, start_ref, gathered, packed, landed, lower, upper, small_sem, *rest = rest
+    load_sem, gather_send, gather_recv, move_send, move_recv, rim_send, rim_recv = rest
+    row_scale_ref, stiffness_ref, base_ref, friction_ref, damping_ref = held_here[:5]
+    deficit_ref, state_ref, obs_rate_ref, obs_precision_ref = held_here[5:]
     member = lax.axis_index("member")
     patch = lax.axis_index("patch")
     members, own = deficit_ref.shape
@@ -72,6 +54,12 @@
     sub_block = own // groups
     last = groups - 1
 
+    small = [
+        pltpu.make_async_copy(source, here, small_sem.at[i])
+        for i, (source, here) in enumerate(zip(sources, held_here))
+    ]
+    for copy in small:
+        copy.start()
     load = pltpu.make_async_copy(kernel_hbm, kernel_ref, load_sem)
     load.start()
 
@@ -79,8 +67,6 @@
     lower[...] = jnp.zeros_like(lower)
     upper[...] = jnp.zeros_like(upper)
     start_ref[...] = jnp.zeros_like(start_ref)
-    start_ref[0, 0:members] = deficit_ref[...]
-    start_ref[1, 0:members] = state_ref[...]
 
     barrier = pltpu.get_barrier_semaphore()
 
@@ -116,6 +102,11 @@
     def _():
         for other in range(groups):
             greet((other, after))
+
+    for copy in small:
+        copy.wait()
+    start_ref[0, 0:members] = deficit_ref[...]
+    start_ref[1, 0:members] = state_ref[...]
 
     rims = has_after + has_before + groups * (takes_lower + takes_upper)
     pl.semaphore_wait(barrier, count + groups - 2 + rims)
@@ -144,8 +135,9 @@
         return target(shift)
 
     stage = [0]
-
-    def stress_of(deficit):
+    pending = []
+
+    def stress_of(deficit, meanwhile=None):
         slot = stage[0] % 2
         mine = gathered.at[slot, patch, 0:members]
         gathered[slot, patch] = deficit.astype(jnp.bfloat16)
@@ -161,6 +153,9 @@
             )
             copy.start()
             copies.append(copy)
+        pending.append(copies)
+        if meanwhile is not None:
+            meanwhile()
         if stage[0] == 0:
             load.wait()
         summed = jnp.zeros((rows, own), jnp.float32)
@@ -183,15 +178,15 @@
                 (((1,), (1,)), ((), ())),
                 preferred_element_type=jnp.float32,
             )
-        for copy in copies:
-            copy.wait_send()
+        while len(pending) > 1 or (pending and stage[0] == 3 * STEPS):
+            for copy in pending.pop(0):
+                copy.wait_send()
         stage[0] += 1
         return base + stiffness * deficit + row_scale * summed
 
-    def rate(deficit, state_log, guess):
-        return slip_rate(
-            stress_of(deficit), state_log, guess, friction, inverse_friction, damping
-        )
+    def rate(deficit, state_log, guess, meanwhile=None):
+        stress = stress_of(deficit, meanwhile)
+        return slip_rate(stress, state_log, guess, friction, inverse_friction, damping)
 
     def tendency(deficit, state_log, guess):
         velocity = rate(deficit, state_log, guess)
@@ -211,30 +206,35 @@
         change, state_change, velocity = tendency(deficit_two, state_two, velocity)
         deficit = deficit_zero / 3.0 + 2.0 / 3.0 * (deficit_two + time_step * change)
         state_log = state_zero / 3.0 + 2.0 / 3.0 * (state_two + time_step * state_change)
-    velocity = rate(deficit, state_log, velocity)
+    def window(cells, first):
+        return pltpu.roll(cells, (-first) % own, 1)[:, :LANES]
+
+    def move(which, shift):
+        lo, size = (0, rows) if which == 0 else (rows, 2 * rows)
+        other = lax.rem(member + shift, groups)
+        return pltpu.make_async_remote_copy(
+            src_ref=packed.at[other, lo : lo + size],
+            dst_ref=landed.at[shift, lo : lo + size],
+            send_sem=move_send.at[which, shift],
+            recv_sem=move_recv.at[which, shift],
+            device_id=(other, patch),
+            device_id_type=MESH,
+        )
+
+    def send_states():
+        for group in range(groups):
+            packed[group, rows : 2 * rows] = window(deficit, group * sub_block)
+            packed[group, 2 * rows :] = window(state_log, group * sub_block)
+        for shift in range(1, groups):
+            move(1, shift).start()
+
+    velocity = rate(deficit, state_log, velocity, send_states)
 
     row = lax.broadcasted_iota(jnp.int32, (rows, own), 0)
     joined = jnp.where(row == members, obs_rate_ref[...], velocity)
     joined = jnp.where(row == members + 1, obs_precision_ref[...], joined)
-
-    def window(cells, first):
-        return pltpu.roll(cells, (-first) % own, 1)[:, :LANES]
-
     for group in range(groups):
         packed[group, 0:rows] = window(joined, group * sub_block - MARGIN)
-        packed[group, rows : 2 * rows] = window(deficit, group * sub_block)
-        packed[group, 2 * rows :] = window(state_log, group * sub_block)
-
-    def move(shift):
-        other = lax.rem(member + shift, groups)
-        return pltpu.make_async_remote_copy(
-            src_ref=packed.at[other],
-            dst_ref=landed.at[shift],
-            send_sem=move_send.at[shift],
-            recv_sem=move_recv.at[shift],
-            device_id=(other, patch),
-            device_id_type=MESH,
-        )
 
     def right_rim():
         return pltpu.make_async_remote_copy(
@@ -265,7 +265,7 @@
         left_rim().start()
 
     for shift in range(1, groups):
-        move(shift).start()
+        move(0, shift).start()
 
     landed[0] = packed[member]
 
@@ -294,7 +294,8 @@
             ).wait_recv()
 
     for shift in range(1, groups):
-        move(shift).wait_recv()
+        move(1, shift).wait_recv()
+        move(0, shift).wait_recv()
 
     lane = lax.broadcasted_iota(jnp.int32, (rows, LANES), 1)
     below = jnp.logical_and(lane < MARGIN, member == 0)
@@ -312,7 +313,8 @@
         fields_out[other, 2] = held[2 * rows :]
 
     for shift in range(1, groups):
-        move(shift).wait_send()
+        move(1, shift).wait_send()
+        move(0, shift).wait_send()
 
     @pl.when(has_after > 0)
     def _():
@@ -502,9 +504,12 @@
     fields = pl.pallas_call(
         functools.partial(forecast_kernel, groups, count),
         out_shape=jax.ShapeDtypeStruct((groups, 3, rows, LANES), f32),
-        in_specs=[pl.BlockSpec(memory_space=pl.ANY)] + [vmem] * 9,
+        in_specs=[pl.BlockSpec(memory_space=pl.ANY)] * 10,
         out_specs=vmem,
-        scratch_shapes=[
+        scratch_shapes=[pltpu.VMEM((1, own), f32)] * 5
+        + [pltpu.VMEM((members, own), f32)] * 2
+        + [pltpu.VMEM((1, own), f32)] * 2
+        + [
             pltpu.VMEM((own, patches), jnp.bfloat16),
             pltpu.VMEM((2, rows, own), f32),
             pltpu.VMEM((2, count, rows, own), jnp.bfloat16),
@@ -512,11 +517,12 @@
             pltpu.VMEM((groups, 3 * rows, LANES), f32),
             pltpu.VMEM((groups, rows, LANES), f32),
             pltpu.VMEM((groups, rows, LANES), f32),
+            pltpu.SemaphoreType.DMA((9,)),
             pltpu.SemaphoreType.DMA,
             pltpu.SemaphoreType.DMA((2, count)),
             pltpu.SemaphoreType.DMA((2, count)),
-            pltpu.SemaphoreType.DMA((groups,)),
-            pltpu.SemaphoreType.DMA((groups,)),
+            pltpu.SemaphoreType.DMA((2, groups)),
+            pltpu.SemaphoreType.DMA((2, groups)),
             pltpu.SemaphoreType.DMA((2,)),
             pltpu.SemaphoreType.DMA((2, groups)),
         ],

time: 45.2 us -> 44.4 us (0.982)
  Pallas kernels: 45 us -> 44.2 us
    pallas_call x1, Pallas kernels: 40.1 us -> 39.3 us  [body(): pl.pallas_call(functools.partial(forecast_kernel, groups, count), out_sha...]
where the time goes in v3:
time: 44.4 us; the launch traced here: 44.3 us
  Pallas kernels  44.2 us (100%)
    pallas_call x1, Pallas kernels, body(): pl.pallas_call(functools.partial(forecast_kernel, groups, count), out_sha...  39.3 us
    pallas_call x1, Pallas kernels, body(): pl.pallas_call(functools.partial(analysis_kernel, members, sub_block), ou...  4.93 us

profile of v3, /device:TPU:0, one launch (start us, length us, event | category | flops | bytes accessed | tf_op | source)
XLA Modules:
  0.0 44.3 jit_solution(8322098017871263917)
XLA Ops:
  0.0 39.3 %shard_map.100.fields_ref = f32[4,3,8,128]{3,2,1,0:T(8,128)} custom-call(bf16[256,2048]{1,0:T(8,128)(2,1)} %kernel_hbm.1, f32[1,256]{1,0:T(1,128)} %bitcast.10, f32[1,256]{1,0:T(1,128)} %bitcast.11, f32[1,256]{1,0:T(1,128)} %bitcast.12, f32[1,256]{1,0:T(1,128)} %bitcast.13, f32[1,256]{1,0:T(1,128)} %bitcast.14, f32[6,256]{1,0:T(8,128)} %rest_5_.1, ...), custom_call_target="tpu_custom_call" | custom-call | tf_op jit(solution)/shard_map/pallas_call | solution.py:504
  39.3 4.9 %shard_map.101 = f32[3,24,64]{2,1,0:T(8,128)} custom-call(f32[4,3,8,128]{3,2,1,0:T(8,128)} %shard_map.100.fields_ref), custom_call_target="tpu_custom_call" | custom-call | tf_op jit(solution)/shard_map/pallas_call | solution.py:545
